TPU v7x, 32 devices: a whole 2x2x4 slice. The times are simulated.
32 devices in a mesh: region: 4 (over x, core), tile: 8 (over z, y).
Axes of the slice: x: 2, y: 2, z: 4, core: 2. Of those that a mesh axis runs over, the one named last changes fastest.
Arguments:
- quantized: bfloat16 [131072, 1024], P(('region', 'tile')), may hold values from -6 to 6
- block_scales: float32 [8, 131072], P(None, ('region', 'tile')), may hold values from 0.25 to 4
- band_width: int32 [32], replicated, may hold values from 1 to 256, as said below
- valid_count: int32 [32], P(('region', 'tile')), may hold values from 1024 to 4096, as said below
- prior_basis: float32 [1024, 64], replicated, may hold values from -0.1875 to 0.1875
Outputs:
- projected: float32 [64, 131072], P(None, ('region', 'tile'))
- new_basis: float32 [1024, 64], replicated
Inputs may be any that keep to these rules, and one draw needn't show every extreme that they name: `band_width`: some tile other than the first of its region has width 256 in every draw. `valid_count`: the last tile's count is 4096 in every draw.
All inputs are finite; a program needn't handle non-finite values.
Results may differ from a plain program's by a relative error of at most 0.0016.
Values may be sent and summed in bfloat16 or wider, within the bound.
A program may use at most 128 MiB of HBM per device.

v0:
```python
import jax
import jax.numpy as jnp
from jax import lax
from jax.sharding import PartitionSpec as P

BAND = 256


def padded_2(cells, sides, width):
    for axis, dim in sides:
        count = lax.axis_size(axis)
        ends = count - 1
        head = lax.slice_in_dim(cells, 0, width, axis=dim)
        tail = lax.slice_in_dim(cells, cells.shape[dim] - width, cells.shape[dim], axis=dim)
        cells = jnp.concatenate(
            [
                lax.ppermute(tail, axis, [(i, (i + 1) % count) for i in range(ends)]),
                cells,
                lax.ppermute(head, axis, [((i + 1) % count, i) for i in range(ends)]),
            ],
            axis=dim,
        )
    return cells


def dequantize(quantized, block_scales):
    tok_rows, feat_dim = quantized.shape
    groups = block_scales.shape[0]
    blocks = (
        quantized.astype(jnp.float32).reshape(tok_rows, groups, feat_dim // groups)
        * block_scales.T[:, :, None]
    )
    return blocks.reshape(tok_rows, feat_dim).astype(jnp.bfloat16)


def blend(initial, neighbour, chosen):
    summed = (initial.astype(jnp.float32) + neighbour.astype(jnp.float32)) * 0.5
    return jnp.where(chosen[:, None], summed, initial.astype(jnp.float32)).astype(jnp.bfloat16)


def finish(update, cross_sum, centred, spread):
    factor = jnp.linalg.cholesky(cross_sum)
    own_basis = jax.scipy.linalg.solve_triangular(factor, update.T, lower=True).T
    new_basis = spread(own_basis)
    projected = lax.dot_general(
        new_basis, centred, (((0,), (1,)), ((), ())), precision=lax.Precision.HIGHEST
    )
    return (projected, new_basis)


def per_device(quantized, block_scales, band_width, valid_count, prior_basis):
    tok_rows, feat_dim = quantized.shape
    n_region = lax.axis_size("region")
    n_tile = lax.axis_size("tile")
    devices = n_region * n_tile
    region_index = lax.axis_index("region")
    tile_index = lax.axis_index("tile")
    tile_number = region_index * n_tile + tile_index
    restored = dequantize(quantized, block_scales)
    padded = padded_2(restored, (("tile", 0),), BAND)
    prev_tail = padded[:BAND]
    next_head = padded[tok_rows + BAND :]
    left_width = jnp.where(tile_index > 0, band_width[tile_number], 0)
    right_width = jnp.where(
        tile_index < n_tile - 1, band_width[jnp.minimum(tile_number + 1, devices - 1)], 0
    )
    positions = jnp.arange(BAND)
    blank = jnp.zeros((BAND, feat_dim), jnp.bfloat16)
    left_part = lax.dynamic_slice_in_dim(
        jnp.concatenate([prev_tail, blank], 0), BAND - left_width, BAND, 0
    )
    right_part = lax.dynamic_slice_in_dim(
        jnp.concatenate([blank, next_head], 0), right_width, BAND, 0
    )
    new_head = blend(restored[:BAND], left_part, positions < left_width)
    new_tail = blend(restored[tok_rows - BAND :], right_part, positions >= BAND - right_width)
    blended = jnp.concatenate([new_head, restored[BAND : tok_rows - BAND], new_tail], 0)
    usable = jnp.arange(tok_rows) < valid_count[0]
    masked = jnp.where(usable[:, None], blended, jnp.zeros((), jnp.bfloat16))
    indicator = jnp.ones((tok_rows,), jnp.bfloat16)
    local_sums = jnp.dot(indicator, masked, preferred_element_type=jnp.float32)
    local_count = valid_count[0].astype(jnp.float32)
    masked_wide = masked.astype(jnp.float32)
    reduced = jnp.dot(masked_wide, prior_basis, precision=lax.Precision.HIGHEST)
    local_update = lax.dot_general(
        masked_wide, reduced, (((0,), (0,)), ((), ())), precision=lax.Precision.HIGHEST
    )
    summed_update, feature_sums, token_count = lax.psum(
        (local_update, local_sums, local_count), ("region", "tile")
    )
    average = feature_sums / token_count
    mean_image = jnp.dot(average, prior_basis, precision=lax.Precision.HIGHEST)
    update = summed_update - jnp.outer(feature_sums, mean_image)
    centred = jnp.where(usable[:, None], masked_wide - average, 0.0)
    cross_sum = jnp.dot(update.T, update, precision=lax.Precision.HIGHEST)
    return finish(update, cross_sum, centred, lambda block: block)


def solution(mesh):
    return jax.shard_map(
        per_device,
        mesh=mesh,
        in_specs=(
            P(("region", "tile"), None),
            P(None, ("region", "tile")),
            P(),
            P(("region", "tile")),
            P(),
        ),
        out_specs=(P(None, ("region", "tile")), P()),
        check_vma=False,
    )
```

profile of v0, /device:TPU:0, one launch (start us, length us, event | category | flops | bytes accessed | tf_op | source)
XLA Modules:
  0.0 243.6 jit_solution(15910361438467005526)
XLA Ops:
  7.2 0.0 copy-start
  7.2 0.0 all-reduce.5.cloned.1.call-start
  7.2 1.5 copy.7
  8.8 4.6 %mul.34 = f32[4096,8,128]{2,1,0:T(8,128)S(1)} broadcast(f32[4096,8]{1,0:T(8,128)S(1)} %copy.7), dimensions={0,1} | broadcast | bytes 16908288 | tf_op jit(solution)/shard_map/mul | solution.py:30
  13.4 7.7 %fusion = bf16[4096,1024]{1,0:T(8,128)(2,1)S(1)} fusion(f32[512,8,8,128]{3,2,1,0:T(8,128)S(1)} %bitcast.33, bf16[4096,1024]{1,0:T(8,128)(2,1)} %param.5), kind=kLoop, calls=%fused_computation.1 | loop fusion | flops 12582912 | bytes 33554432 | tf_op jit(solution)/shard_map/convert_element_type | solution.py:33
  21.1 3.2 %copy-done.2 = bf16[4096,1024]{1,0:T(8,128)(2,1)} copy-done((bf16[4096,1024]{1,0:T(8,128)(2,1)}, bf16[4096,1024]{1,0:T(8,128)(2,1)S(1)}, u32[]{:S(2)}) %copy-start.2) | copy-done | bytes 8388632
  24.3 0.1 fusion.25
  24.4 4.9 %collective-permute-start = (bf16[256,1024]{1,0:T(8,128)(2,1)S(1)}, bf16[256,1024]{1,0:T(8,128)(2,1)S(1)}, u32[]{:S(2)}, u32[]{:S(2)}) collective-permute-start(bf16[256,1024]{1,0:T(8,128)(2,1)S(1)} %get-tuple-element.6), channel_id=1, source_target_pairs={{0,1},{1,2},{2,3},{3,4},{4,5},{5,6},{6,7},{8,9},{9,10},{10,11},{11... | collective-permute-start | bytes 1572872 | tf_op jit(solution)/shard_map/ppermute | solution.py:17
  29.3 1.3 collective-permute-start.1
  30.7 6.9 %slice.28 = bf16[3584,1024]{1,0:T(8,128)(2,1)} slice(bf16[4096,1024]{1,0:T(8,128)(2,1)} %copy-done.2), slice={[256:3840], [0:1024]} | slice | bytes 14680064 | tf_op jit(solution)/shard_map/slice | solution.py:77
  37.6 0.6 fusion.26
  40.2 11.5 %collective-permute-done = bf16[256,1024]{1,0:T(8,128)(2,1)S(1)} collective-permute-done((bf16[256,1024]{1,0:T(8,128)(2,1)S(1)}, bf16[256,1024]{1,0:T(8,128)(2,1)S(1)}, u32[]{:S(2)}, u32[]{:S(2)}) %collective-permute-start) | collective-permute-done | bytes 524320 | tf_op jit(solution)/shard_map/ppermute | solution.py:17
  51.7 0.0 collective-permute-done.1
  51.7 1.8 fusion.9
  53.6 6.2 %maximum_select_fusion = bf16[4096,1024]{1,0:T(8,128)(2,1)S(1)} fusion(bf16[256,1024]{1,0:T(8,128)(2,1)S(1)} %get-tuple-element.5, bf16[3584,1024]{1,0:T(8,128)(2,1)} %slice.28, bf16[256,1024]{1,0:T(8,128)(2,1)S(1)} %get-tuple-element.4, pred[4096]{0:T(1024)(128)(4,1)S(1)} %iota_compare_fusion.2), kind=kLoop, calls=%fused_computation.6 | loop fusion | flops 29360128 | bytes 16781312 | tf_op jit(solution)/shard_map/jit(_where)/select_n | solution.py:79
  59.8 1.2 fusion.21
  61.0 6.7 %fusion.27 = f32[4096,64]{1,0:T(8,128)S(1)} fusion(bf16[4096,1024]{1,0:T(8,128)(2,1)S(1)} %maximum_select_fusion, f32[1024,64]{0,1:T(8,128)S(1)} %copy-done), kind=kOutput, calls=%fused_computation.47 | convolution fusion | flops 3221225472 | bytes 9699328 | tf_op jit(solution)/shard_map/dot_general | solution.py:84
  67.7 5.3 %fusion.28 = f32[1024,64]{0,1:T(8,128)} fusion(bf16[4096,1024]{1,0:T(8,128)(2,1)S(1)} %maximum_select_fusion, f32[4096,64]{1,0:T(8,128)S(1)} %fusion.27), kind=kOutput, calls=%fused_computation.48 | convolution fusion | flops 3221225472 | bytes 9699328 | tf_op jit(solution)/shard_map/dot_general | solution.py:85
  73.0 0.0 all-reduce.5.cloned.1.call-update
  73.0 41.8 %all-reduce.2 = (f32[1024]{0:T(1024)S(1)}, f32[]{:T(128)}) all-reduce(f32[1024]{0:T(1024)S(1)} %bitcast.37, f32[]{:T(128)S(6)} %convert_element_type.40), channel_id=1, replica_groups=mesh['region'=4,'tile'=8] {'region','tile'}, use_global_device_ids=true, to_apply=%region_1.2 | all-reduce | flops 1025 | bytes 8200 | tf_op jit(solution)/shard_map/psum | solution.py:88
  114.7 0.6 broadcast_divide_fusion
  115.4 0.3 convolution_bitcast_fusion
  115.7 86.2 %all-reduce.5.cloned.1.call-done = f32[1024,64]{0,1:T(8,128)} async-done(((f32[1024,64]{0,1:T(8,128)}), f32[1024,64]{0,1:T(8,128)}) %all-reduce.5.cloned.1.call-update) | async-done | bytes 262160 | tf_op jit(solution)/shard_map/psum | solution.py:88
  201.9 1.5 fusion.13
  203.3 0.1 copy.8
  203.4 5.8 %cholesky.16 = f32[64,64]{1,0:T(8,128)S(1)} custom-call(f32[64,64]{1,0:T(8,128)S(1)} %fusion.20), custom_call_target="Cholesky" | custom-call | tf_op jit(solution)/shard_map/jit(cholesky)/cholesky | solution.py:42
  209.3 0.6 compare_reduce_fusion
  210.0 0.7 fusion.18
  210.6 4.9 %custom-call.7 = f32[1,64,64]{1,2,0:T(8,128)S(1)} custom-call(f32[1,64,64]{2,1,0:T(8,128)S(1)} %fusion.18), custom_call_target="InvertDiagBlocksLowerTriangular" | custom-call | tf_op jit(solution)/shard_map/jit(_solve_triangular)/triangular_solve | solution.py:43
  215.5 1.4 fusion.12
  216.9 0.0 copy-start.3
  217.0 19.8 %fusion.1 = f32[64,4096]{1,0:T(8,128)} fusion(f32[64,1024]{1,0:T(8,128)S(1)} %fusion.12, bf16[4096,1024]{1,0:T(8,128)(2,1)} %copy-done.1, f32[1024]{0:T(1024)S(1)} %broadcast_divide_fusion, pred[4096]{0:T(1024)(128)(4,1)S(1)} %iota_compare_fusion.2), kind=kOutput, calls=%fused_computation.2 | convolution fusion | flops 3233808384 | bytes 9707520 | tf_op jit(solution)/shard_map/dot_general | solution.py:45
  (11 shorter events, 0.1 us)
Async XLA Ops:
  7.2 53.9 %copy-start = (f32[1024,64]{0,1:T(8,128)S(1)}, f32[1024,64]{0,1:T(8,128)}, u32[]{:S(2)}) copy-start(f32[1024,64]{0,1:T(8,128)} %param.9) | copy-start | bytes 786436
  7.2 194.7 %all-reduce.5.cloned.1.call-start = ((), (), s32[]{:S(2)}) async-start(), calls=%async_computation | async-start | bytes 524288 | tf_op jit(solution)/shard_map/psum | solution.py:88
  21.1 3.2 %copy-start.2 = (bf16[4096,1024]{1,0:T(8,128)(2,1)}, bf16[4096,1024]{1,0:T(8,128)(2,1)S(1)}, u32[]{:S(2)}) copy-start(bf16[4096,1024]{1,0:T(8,128)(2,1)S(1)} %fusion) | copy-start | bytes 25165828
  24.3 13.3 %copy-start.4 = (s32[32]{0:T(128)S(1)}, s32[32]{0:T(128)}, u32[]{:S(2)}) copy-start(s32[32]{0:T(128)} %param.7) | copy-start | bytes 388
  24.4 27.3 %collective-permute-start = (bf16[256,1024]{1,0:T(8,128)(2,1)S(1)}, bf16[256,1024]{1,0:T(8,128)(2,1)S(1)}, u32[]{:S(2)}, u32[]{:S(2)}) collective-permute-start(bf16[256,1024]{1,0:T(8,128)(2,1)S(1)} %get-tuple-element.6), channel_id=1, source_target_pairs={{0,1},{1,2},{2,3},{3,4},{4,5},{5,6},{6,7},{8,9},{9,10},{10,11},{11... | collective-permute-start | bytes 1572872 | tf_op jit(solution)/shard_map/ppermute | solution.py:17
  29.3 22.4 %collective-permute-start.1 = (bf16[256,1024]{1,0:T(8,128)(2,1)S(1)}, bf16[256,1024]{1,0:T(8,128)(2,1)S(1)}, u32[]{:S(2)}, u32[]{:S(2)}) collective-permute-start(bf16[256,1024]{1,0:T(8,128)(2,1)S(1)} %get-tuple-element.7), channel_id=1, source_target_pairs={{1,0},{2,1},{3,2},{4,3},{5,4},{6,5},{7,6},{9,8},{10,9},{11,10},{12... | collective-permute-start | bytes 1572872 | tf_op jit(solution)/shard_map/ppermute | solution.py:19
  59.8 7.9 %copy-start.1 = (bf16[4096,1024]{1,0:T(8,128)(2,1)}, bf16[4096,1024]{1,0:T(8,128)(2,1)S(1)}, u32[]{:S(2)}) copy-start(bf16[4096,1024]{1,0:T(8,128)(2,1)S(1)} %maximum_select_fusion) | copy-start | bytes 25165828
  216.9 19.8 %copy-start.3 = (f32[64,1024]{1,0:T(8,128)}, f32[64,1024]{1,0:T(8,128)S(1)}, u32[]{:S(2)}) copy-start(f32[64,1024]{1,0:T(8,128)S(1)} %fusion.12) | copy-start | bytes 786436
Sparse Core Ops, SparseCore 0:
  73.1 128.7 all-reduce.4
where the time goes:
time: 244 us
  waiting for transfers between devices  97.8 us (40%)
  blocking collectives  41.8 us (17%)
  matrix products  36.1 us (15%)
  other arithmetic  28.6 us (12%)
  local copies, waits for them, and re-layouts  17 us (7%)
  between operations  16.2 us (7%)
  starting transfers between devices  6.26 us (3%)
    psum x1, waiting for transfers between devices, per_device(): lax.psum((local_update, local_sums, local_count), ('region', 'tile'))  86.2 us
    psum x1, blocking collectives, per_device(): lax.psum((local_update, local_sums, local_count), ('region', 'tile'))  41.8 us
    dot_general x1, matrix products, finish(): lax.dot_general(new_basis, centred, (((0,), (1,)), ((), ())), precision=l...  19.8 us
    ppermute x1, waiting for transfers between devices, padded_2(): lax.ppermute(tail, axis, [(i, (i + 1) % count) for i in range(ends)])  11.5 us
    convert_element_type x1, other arithmetic, dequantize(): return blocks.reshape(tok_rows, feat_dim).astype(jnp.bfloat16)  7.73 us
    slice x1, local copies, waits for them, and re-layouts, per_device(): restored[BAND:tok_rows - BAND]  6.93 us
    dot_general x1, matrix products, per_device(): reduced = jnp.dot(masked_wide, prior_basis, precision=lax.Precision.HIGHEST)  6.67 us
    another operation x3, other arithmetic, finish(): factor = jnp.linalg.cholesky(cross_sum)  6.52 us
  transfers between devices with their start and end apart: 3, of which 2 were waited for; matrix products, arithmetic and copies ran while one was open for 3% of the time, Pallas kernels for 0%

commit v1 on v0

--- a/solution.py
+++ b/solution.py
@@ -86,7 +86,7 @@
         masked_wide, reduced, (((0,), (0,)), ((), ())), precision=lax.Precision.HIGHEST
     )
     summed_update, feature_sums, token_count = lax.psum(
-        (local_update, local_sums, local_count), ("region", "tile")
+        lax.psum((local_update, local_sums, local_count), "tile"), "region"
     )
     average = feature_sums / token_count
     mean_image = jnp.dot(average, prior_basis, precision=lax.Precision.HIGHEST)

time: 244 us -> 221 us (0.906)
  waiting for transfers between devices: 97.8 us -> 83.8 us
  blocking collectives: 41.8 us -> 29.2 us
  matrix products: 36.1 us -> 39.4 us
    psum x1 -> x2, waiting for transfers between devices: 86.2 us -> 72.2 us  [the longest x1 39.3 us: per_device(): lax.psum((local_update, local_sums, local_count), 'tile')]
    psum x1 -> x2, blocking collectives: 41.8 us -> 29.2 us  [the longest x1 22.4 us: per_device(): lax.psum((local_update, local_sums, local_count), 'tile')]
    dot_general x1, matrix products: 1.19 us -> 4.57 us  [per_device(): local_sums = jnp.dot(indicator, masked, preferred_element_type=jnp.float32)]
  transfers between devices with their start and end apart: 3 -> 4, of which waited for: 2 -> 3; matrix products, arithmetic and copies ran while one was open for 3% -> 6% of each run, Pallas kernels for 0% -> 0%
where the time goes in v1:
time: 221 us
  waiting for transfers between devices  83.8 us (38%)
  matrix products  39.4 us (18%)
  blocking collectives  29.2 us (13%)
  other arithmetic  28.6 us (13%)
  local copies, waits for them, and re-layouts  17 us (8%)
  between operations  16.2 us (7%)
  starting transfers between devices  6.52 us (3%)
    psum x1, waiting for transfers between devices, per_device(): lax.psum((local_update, local_sums, local_count), 'tile')  39.3 us
    psum x1, waiting for transfers between devices, per_device(): lax.psum(lax.psum((local_update, local_sums, local_count), 'tile'), 'regi...  32.9 us
    psum x1, blocking collectives, per_device(): lax.psum((local_update, local_sums, local_count), 'tile')  22.4 us
    dot_general x1, matrix products, finish(): lax.dot_general(new_basis, centred, (((0,), (1,)), ((), ())), precision=l...  19.8 us
    ppermute x1, waiting for transfers between devices, padded_2(): lax.ppermute(tail, axis, [(i, (i + 1) % count) for i in range(ends)])  11.5 us
    convert_element_type x1, other arithmetic, dequantize(): return blocks.reshape(tok_rows, feat_dim).astype(jnp.bfloat16)  7.73 us
    slice x1, local copies, waits for them, and re-layouts, per_device(): restored[BAND:tok_rows - BAND]  6.94 us
    psum x1, blocking collectives, per_device(): lax.psum(lax.psum((local_update, local_sums, local_count), 'tile'), 'regi...  6.77 us
  transfers between devices with their start and end apart: 4, of which 3 were waited for; matrix products, arithmetic and copies ran while one was open for 6% of the time, Pallas kernels for 0%

profile of v1, /device:TPU:0, one launch (start us, length us, event | category | flops | bytes accessed | tf_op | source)
XLA Modules:
  0.0 220.7 jit_solution(13792028329443223035)
XLA Ops:
  7.2 0.0 all-reduce.7.cloned.1.call-start
  7.2 1.5 copy.7
  8.8 4.6 %mul.34 = f32[4096,8,128]{2,1,0:T(8,128)S(1)} broadcast(f32[4096,8]{1,0:T(8,128)S(1)} %copy.7), dimensions={0,1} | broadcast | bytes 16908288 | tf_op jit(solution)/shard_map/mul | solution.py:30
  13.4 7.7 %fusion = bf16[4096,1024]{1,0:T(8,128)(2,1)S(1)} fusion(f32[512,8,8,128]{3,2,1,0:T(8,128)S(1)} %bitcast.33, bf16[4096,1024]{1,0:T(8,128)(2,1)} %param.5), kind=kLoop, calls=%fused_computation.1 | loop fusion | flops 12582912 | bytes 33554432 | tf_op jit(solution)/shard_map/convert_element_type | solution.py:33
  21.1 3.2 %copy-done.2 = bf16[4096,1024]{1,0:T(8,128)(2,1)} copy-done((bf16[4096,1024]{1,0:T(8,128)(2,1)}, bf16[4096,1024]{1,0:T(8,128)(2,1)S(1)}, u32[]{:S(2)}) %copy-start.2) | copy-done | bytes 8388632
  24.3 0.1 fusion.25
  24.4 4.9 %collective-permute-start = (bf16[256,1024]{1,0:T(8,128)(2,1)S(1)}, bf16[256,1024]{1,0:T(8,128)(2,1)S(1)}, u32[]{:S(2)}, u32[]{:S(2)}) collective-permute-start(bf16[256,1024]{1,0:T(8,128)(2,1)S(1)} %get-tuple-element.8), channel_id=1, source_target_pairs={{0,1},{1,2},{2,3},{3,4},{4,5},{5,6},{6,7},{8,9},{9,10},{10,11},{11... | collective-permute-start | bytes 1572872 | tf_op jit(solution)/shard_map/ppermute | solution.py:17
  29.3 1.3 collective-permute-start.1
  30.7 6.9 %slice.28 = bf16[3584,1024]{1,0:T(8,128)(2,1)} slice(bf16[4096,1024]{1,0:T(8,128)(2,1)} %copy-done.2), slice={[256:3840], [0:1024]} | slice | bytes 14680064 | tf_op jit(solution)/shard_map/slice | solution.py:77
  37.6 0.6 fusion.26
  40.2 11.5 %collective-permute-done = bf16[256,1024]{1,0:T(8,128)(2,1)S(1)} collective-permute-done((bf16[256,1024]{1,0:T(8,128)(2,1)S(1)}, bf16[256,1024]{1,0:T(8,128)(2,1)S(1)}, u32[]{:S(2)}, u32[]{:S(2)}) %collective-permute-start) | collective-permute-done | bytes 524320 | tf_op jit(solution)/shard_map/ppermute | solution.py:17
  51.7 1.8 fusion.9
  53.6 6.2 %maximum_select_fusion = bf16[4096,1024]{1,0:T(8,128)(2,1)S(1)} fusion(bf16[256,1024]{1,0:T(8,128)(2,1)S(1)} %get-tuple-element.7, bf16[3584,1024]{1,0:T(8,128)(2,1)} %slice.28, bf16[256,1024]{1,0:T(8,128)(2,1)S(1)} %get-tuple-element.6, pred[4096]{0:T(1024)(128)(4,1)S(1)} %iota_compare_fusion.2), kind=kLoop, calls=%fused_computation.6 | loop fusion | flops 29360128 | bytes 16781312 | tf_op jit(solution)/shard_map/jit(_where)/select_n | solution.py:79
  59.8 6.7 %fusion.27 = f32[4096,64]{1,0:T(8,128)S(1)} fusion(bf16[4096,1024]{1,0:T(8,128)(2,1)S(1)} %maximum_select_fusion, f32[1024,64]{0,1:T(8,128)S(1)} %copy-done), kind=kOutput, calls=%fused_computation.47 | convolution fusion | flops 3221225472 | bytes 9699328 | tf_op jit(solution)/shard_map/dot_general | solution.py:84
  66.5 5.3 %fusion.28 = f32[1024,64]{0,1:T(8,128)} fusion(bf16[4096,1024]{1,0:T(8,128)(2,1)S(1)} %maximum_select_fusion, f32[4096,64]{1,0:T(8,128)S(1)} %fusion.27), kind=kOutput, calls=%fused_computation.48 | convolution fusion | flops 3221225472 | bytes 9699328 | tf_op jit(solution)/shard_map/dot_general | solution.py:85
  71.8 0.0 all-reduce.7.cloned.1.call-update
  71.8 0.3 all-reduce.9.cloned.1.call-start
  72.1 4.6 %fusion.21 = f32[1,1024]{1,0:T(1,128)S(1)} fusion(bf16[4096,1024]{1,0:T(8,128)(2,1)} %copy-done.1), kind=kOutput, calls=%fused_computation.37 | convolution fusion | flops 8388608 | bytes 8392704 | tf_op jit(solution)/shard_map/dot_general | solution.py:81
  76.6 22.4 %all-reduce.2 = (f32[1024]{0:T(1024)S(1)}, f32[]{:T(128)}) all-reduce(f32[1024]{0:T(1024)S(1)} %bitcast.37, f32[]{:T(128)S(6)} %convert_element_type.40), channel_id=1, replica_groups=mesh['region'=4,'tile'=8] {'tile'}, use_global_device_ids=true, to_apply=%region_2.3 | all-reduce | flops 1025 | bytes 8200 | tf_op jit(solution)/shard_map/psum | solution.py:89
  99.0 6.8 %all-reduce.3 = (f32[1024]{0:T(1024)S(1)}, f32[]{:T(128)}) all-reduce(f32[1024]{0:T(1024)S(1)} %get-tuple-element.2, f32[]{:T(128)} %get-tuple-element.3), channel_id=1, replica_groups=mesh['region'=4,'tile'=8] {'region'}, use_global_device_ids=true, to_apply=%region_3.4 | all-reduce | flops 1025 | bytes 8200 | tf_op jit(solution)/shard_map/psum | solution.py:88
  105.8 39.3 %all-reduce.7.cloned.1.call-done = f32[1024,64]{0,1:T(8,128)} async-done(((f32[1024,64]{0,1:T(8,128)}), f32[1024,64]{0,1:T(8,128)}) %all-reduce.7.cloned.1.call-update) | async-done | bytes 262160 | tf_op jit(solution)/shard_map/psum | solution.py:89
  145.2 0.7 broadcast_divide_fusion
  145.8 0.3 convolution_bitcast_fusion
  146.1 32.9 %all-reduce.9.cloned.1.call-done = f32[1024,64]{0,1:T(8,128)} async-done(((f32[1024,64]{0,1:T(8,128)}), f32[1024,64]{0,1:T(8,128)}) %all-reduce.9.cloned.1.call-update) | async-done | bytes 262160 | tf_op jit(solution)/shard_map/psum | solution.py:88
  179.0 1.5 fusion.13
  180.5 0.1 copy.8
  180.6 5.8 %cholesky.16 = f32[64,64]{1,0:T(8,128)S(1)} custom-call(f32[64,64]{1,0:T(8,128)S(1)} %fusion.20), custom_call_target="Cholesky" | custom-call | tf_op jit(solution)/shard_map/jit(cholesky)/cholesky | solution.py:42
  186.4 0.6 compare_reduce_fusion
  187.1 0.7 fusion.18
  187.7 4.9 %custom-call.7 = f32[1,64,64]{1,2,0:T(8,128)S(1)} custom-call(f32[1,64,64]{2,1,0:T(8,128)S(1)} %fusion.18), custom_call_target="InvertDiagBlocksLowerTriangular" | custom-call | tf_op jit(solution)/shard_map/jit(_solve_triangular)/triangular_solve | solution.py:43
  192.6 1.4 fusion.12
  194.1 19.8 %fusion.1 = f32[64,4096]{1,0:T(8,128)} fusion(f32[64,1024]{1,0:T(8,128)S(1)} %fusion.12, bf16[4096,1024]{1,0:T(8,128)(2,1)} %copy-done.1, f32[1024]{0:T(1024)S(1)} %broadcast_divide_fusion, pred[4096]{0:T(1024)(128)(4,1)S(1)} %iota_compare_fusion.2), kind=kOutput, calls=%fused_computation.2 | convolution fusion | flops 3233808384 | bytes 9707520 | tf_op jit(solution)/shard_map/dot_general | solution.py:45
  (15 shorter events, 0.1 us)
Async XLA Ops:
  7.2 52.6 %copy-start = (f32[1024,64]{0,1:T(8,128)S(1)}, f32[1024,64]{0,1:T(8,128)}, u32[]{:S(2)}) copy-start(f32[1024,64]{0,1:T(8,128)} %param.9) | copy-start | bytes 786436
  7.2 138.0 %all-reduce.7.cloned.1.call-start = ((), (), s32[]{:S(2)}) async-start(), calls=%async_computation | async-start | bytes 524288 | tf_op jit(solution)/shard_map/psum | solution.py:89
  21.1 3.2 %copy-start.2 = (bf16[4096,1024]{1,0:T(8,128)(2,1)}, bf16[4096,1024]{1,0:T(8,128)(2,1)S(1)}, u32[]{:S(2)}) copy-start(bf16[4096,1024]{1,0:T(8,128)(2,1)S(1)} %fusion) | copy-start | bytes 25165828
  24.3 13.3 %copy-start.4 = (s32[32]{0:T(128)S(1)}, s32[32]{0:T(128)}, u32[]{:S(2)}) copy-start(s32[32]{0:T(128)} %param.7) | copy-start | bytes 388
  24.4 27.3 %collective-permute-start = (bf16[256,1024]{1,0:T(8,128)(2,1)S(1)}, bf16[256,1024]{1,0:T(8,128)(2,1)S(1)}, u32[]{:S(2)}, u32[]{:S(2)}) collective-permute-start(bf16[256,1024]{1,0:T(8,128)(2,1)S(1)} %get-tuple-element.8), channel_id=1, source_target_pairs={{0,1},{1,2},{2,3},{3,4},{4,5},{5,6},{6,7},{8,9},{9,10},{10,11},{11... | collective-permute-start | bytes 1572872 | tf_op jit(solution)/shard_map/ppermute | solution.py:17
  29.3 22.4 %collective-permute-start.1 = (bf16[256,1024]{1,0:T(8,128)(2,1)S(1)}, bf16[256,1024]{1,0:T(8,128)(2,1)S(1)}, u32[]{:S(2)}, u32[]{:S(2)}) collective-permute-start(bf16[256,1024]{1,0:T(8,128)(2,1)S(1)} %get-tuple-element.9), channel_id=1, source_target_pairs={{1,0},{2,1},{3,2},{4,3},{5,4},{6,5},{7,6},{9,8},{10,9},{11,10},{12... | collective-permute-start | bytes 1572872 | tf_op jit(solution)/shard_map/ppermute | solution.py:19
  59.8 6.7 %copy-start.1 = (bf16[4096,1024]{1,0:T(8,128)(2,1)}, bf16[4096,1024]{1,0:T(8,128)(2,1)S(1)}, u32[]{:S(2)}) copy-start(bf16[4096,1024]{1,0:T(8,128)(2,1)S(1)} %maximum_select_fusion) | copy-start | bytes 25165828
  71.8 107.2 %all-reduce.9.cloned.1.call-start = ((), (), s32[]{:S(2)}) async-start(), calls=%async_computation.1 | async-start | bytes 524288 | tf_op jit(solution)/shard_map/psum | solution.py:88
  194.1 19.8 %copy-start.3 = (f32[64,1024]{1,0:T(8,128)}, f32[64,1024]{1,0:T(8,128)S(1)}, u32[]{:S(2)}) copy-start(f32[64,1024]{1,0:T(8,128)S(1)} %fusion.12) | copy-start | bytes 786436
Sparse Core Ops, SparseCore 0:
  71.9 73.1 all-reduce.6
  147.5 31.4 all-reduce.8
